TPU v7x, 32 devices: a whole 2x2x4 slice. The times are simulated.
32 devices in a mesh: ctx: 8 (over z, core), head: 4 (over y, x).
Axes of the slice: x: 2, y: 2, z: 4, core: 2. Of those that a mesh axis runs over, the one named last changes fastest.
Arguments:
- q_latent: bfloat16 [1024, 1536], P('ctx', 'head'), may hold values from -72 to 72
- latent_cache: bfloat16 [1024, 576], P('ctx'), may hold values from -6 to 6
- w_q_up: bfloat16 [1536, 3072], P(None, 'head'), may hold values from -0.15625 to 0.15625
- w_kv_up: bfloat16 [512, 4096], P(None, 'head'), may hold values from -0.25 to 0.25
- w_out: bfloat16 [2048, 7168], P('head', 'ctx'), may hold values from -1 to 1
- token_pos: int32 [1024], P('ctx'), may hold values from 0 to 1023, as said below
- start_offset: int32 [1], replicated, may hold values from 0 to 65535
Outputs:
- layer_out: bfloat16 [1024, 7168], P('ctx', 'head')
Inputs may be any that keep to these rules, and one draw needn't show every extreme that they name: `token_pos`: a permutation of 0 to 1023; the 128 tokens of each index of ctx hold consecutive positions in increasing order.
All inputs are finite; a program needn't handle non-finite values.
Results may differ from a plain program's by a relative error of at most 0.035.
Values may be sent and summed in bfloat16 or wider, within the bound.
A program may use at most 64 MiB of HBM per device.

v0:
```python
import functools

import jax
import jax.numpy as jnp
from jax import lax
from jax.experimental import pallas as pl
from jax.experimental.pallas import tpu as pltpu
from jax.sharding import PartitionSpec as P

KVL = 512
NOPE = 128
ROPE = 64
VDIM = 128
LANES = KVL + ROPE

negative_fill = -1e30
softmax_scale = 0.135
rope_base = 10000.0
F32 = jnp.float32
BF16 = jnp.bfloat16
MESH = pl.DeviceIdType.MESH


def dot_t(a, b):
    return lax.dot_general(a, b, (((1,), (1,)), ((), ())), preferred_element_type=F32)


def kernel(
    n_c, n_h, heads, rows,
    qlat, lat, wq, wkv, wout, cos, sin, kpos,
    out,
    wq_v, wkv_v, w2, qbuf, latbuf, posbuf, qa, score, prob, attbuf,
    pa, ra, ta, qa2, pb, rb, tb, qb2, rbuf, zbuf,
    lsem, qs, qr, lzs, lps, latr, xzs, xzr, xps, xpr, pzs, pzr, pps, ppr, ws, wr, ats, atr,
    sa1, va1, sa2, va2, sb1, vb1, sb2, vb2, zs, zr, os_, or_,
):
    n_z = n_c // 2
    piece = rows // n_h
    n_lo = n_h // 2
    width = w2.shape[2]
    q_block = qbuf.shape[2]
    c = lax.axis_index("ctx")
    h = lax.axis_index("head")
    k = lax.rem(c, 2)
    z = lax.div(c, 2)
    partner = c + 1 - 2 * k
    z_of = [lax.rem(z + d, n_z) for d in range(n_z)]
    h_of = [lax.rem(h + e, n_h) for e in range(n_h)]
    hi, lo = lax.div(h, n_lo), lax.rem(h, n_lo)
    lo_of = [lax.rem(lo + e, n_lo) for e in range(n_lo)]
    c_of = [2 * zz + k for zz in z_of]

    def remote(src, dst, ssem, rsem, cc, hh):
        return pltpu.make_async_remote_copy(
            src_ref=src, dst_ref=dst, send_sem=ssem, recv_sem=rsem,
            device_id=(cc, hh), device_id_type=MESH,
        )

    def slot(cc):
        return latbuf.at[cc]

    barrier = pltpu.get_barrier_semaphore()
    for d in range(1, n_z):
        pl.semaphore_signal(barrier, inc=1, device_id=(c_of[d], h), device_id_type=MESH)
    for e in range(1, n_h):
        pl.semaphore_signal(barrier, inc=1, device_id=(c, h_of[e]), device_id_type=MESH)
    pl.semaphore_signal(barrier, inc=1, device_id=(partner, h), device_id_type=MESH)

    local = [
        pltpu.make_async_copy(qlat, qbuf.at[h], lsem.at[0]),
        pltpu.make_async_copy(wq, wq_v, lsem.at[1]),
        pltpu.make_async_copy(wkv, wkv_v, lsem.at[2]),
        pltpu.make_async_copy(lat, slot(c), lsem.at[3]),
        pltpu.make_async_copy(wout, w2.at[k], lsem.at[4]),
    ]
    for copy in local:
        copy.start()
    pl.semaphore_wait(barrier, n_z + n_h - 1)

    third_rows = LANES // 3
    odd = lax.rem(lo, 2)
    pair = hi * n_lo + lo + 1 - 2 * odd
    mine = pl.ds(pl.multiple_of(odd * third_rows, third_rows), third_rows)
    other = pl.ds(pl.multiple_of((1 - odd) * third_rows, third_rows), third_rows)
    both = pl.ds(2 * third_rows, third_rows)
    sends = []

    def send(*args):
        copy = remote(*args)
        copy.start()
        sends.append(copy)

    for e in range(1, n_h):
        send(qlat, qbuf.at[h], qs.at[e], qr.at[h], c, h_of[e])
    for d in range(n_z - 1, 0, -1):
        send(lat.at[mine, :], latbuf.at[c, mine, :], xzs.at[d], xzr.at[z], c_of[d], h)
    for d in range(n_z - 1, 0, -1):
        send(lat.at[both, :], latbuf.at[c, both, :], lzs.at[d], latr.at[c], c_of[d], h)
    send(lat, slot(c), lps.at[0], latr.at[c], partner, h)
    posbuf[k, z] = kpos[...]
    for d in range(1, n_z):
        send(kpos, posbuf.at[k, z], pzs.at[d], pzr.at[z], c_of[d], h)

    for d in range(1, n_z):
        cc = c_of[d]
        remote(lat.at[mine, :], latbuf.at[cc, mine, :], xzs.at[d], xzr.at[z_of[d]], cc, h).wait_recv()
        send(latbuf.at[cc, mine, :], latbuf.at[cc, mine, :], xps.at[d], xpr.at[z_of[d]], c, pair)

    local[0].wait()
    local[1].wait()
    for e in range(1, n_h):
        remote(qlat, qbuf.at[h_of[e]], qs.at[e], qr.at[h_of[e]], c, h_of[e]).wait_recv()
    query = None
    for g in range(n_h):
        term = jnp.dot(qbuf[g], wq_v[g * q_block:(g + 1) * q_block, :], preferred_element_type=F32)
        query = term if query is None else query + term
    local[2].wait()
    for j in range(heads):
        base = j * (NOPE + ROPE)
        nope = query[:, base:base + NOPE].astype(BF16)
        main = dot_t(nope, wkv_v[:, j * 256:j * 256 + NOPE])
        lines = slice(j * rows, (j + 1) * rows)
        qa[lines, 0:KVL] = main.astype(BF16)
        rope = query[:, base + NOPE:base + NOPE + ROPE]
        half = ROPE // 2
        swapped = jnp.concatenate([rope[:, half:], rope[:, :half]], axis=1)
        rotated = rope * cos[...] + swapped * sin[...]
        qa[lines, KVL:LANES] = rotated.astype(BF16)

    for d in range(1, n_z):
        cc = c_of[d]
        remote(lat.at[both, :], latbuf.at[cc, both, :], lzs.at[d], latr.at[cc], cc, h).wait_recv()
        remote(
            latbuf.at[cc, other, :], latbuf.at[cc, other, :], xps.at[d], xpr.at[z_of[d]], c, pair
        ).wait_recv()
        send(slot(c_of[d]), slot(c_of[d]), lps.at[d], latr.at[c_of[d]], partner, h)
    for d in range(1, n_z):
        remote(kpos, posbuf.at[k, z_of[d]], pzs.at[d], pzr.at[z_of[d]], c_of[d], h).wait_recv()
    send(posbuf.at[k], posbuf.at[k], pps, ppr, partner, h)
    send(wout, w2.at[k], ws, wr, partner, h)
    local[3].wait()
    for d in range(n_z):
        cc = 2 * z_of[d] + 1 - k
        remote(lat, slot(cc), lps.at[d], latr.at[cc], partner, h).wait_recv()

    remote(posbuf.at[1 - k], posbuf.at[1 - k], pps, ppr, partner, h).wait_recv()
    key_pos = jnp.concatenate([posbuf[cc % 2, cc // 2, 0:1, :] for cc in range(n_c)], axis=1)
    latents = jnp.concatenate([latbuf[cc] for cc in range(n_c)], axis=1)
    score[...] = jnp.dot(qa[...], latents, preferred_element_type=F32)
    visible = key_pos <= jnp.transpose(kpos[...])[:, 0:1]
    sums = []
    for j in range(heads):
        lines = slice(j * rows, (j + 1) * rows)
        s = jnp.where(visible, score[lines, :] * softmax_scale, negative_fill)
        largest = jnp.max(s, axis=-1, keepdims=True)
        weights = jnp.where(visible, jnp.exp(s - largest), 0.0)
        sums.append(jnp.sum(weights, axis=-1, keepdims=True))
        prob[lines, :] = weights.astype(BF16)
    summed = dot_t(prob[...], latents[0:KVL, :])
    for j in range(heads):
        normed = (summed[j * rows:(j + 1) * rows, :] / sums[j]).astype(BF16)
        value = jnp.dot(normed, wkv_v[:, j * 256 + NOPE:(j + 1) * 256], preferred_element_type=F32)
        attbuf[z, :, j * VDIM:(j + 1) * VDIM] = value.astype(BF16)

    for d in range(n_z - 1, 0, -1):
        send(attbuf.at[z], attbuf.at[z], ats.at[d], atr.at[z], c_of[d], h)

    local[4].wait()
    remote(wout, w2.at[1 - k], ws, wr, partner, h).wait_recv()

    def project(d):
        zz = z_of[d]
        if d > 0:
            remote(attbuf.at[zz], attbuf.at[zz], ats.at[d], atr.at[zz], c_of[d], h).wait_recv()
        part = jnp.dot(attbuf[zz], w2[0], preferred_element_type=F32).astype(BF16)
        for i in range(n_h):
            pa[d, i % n_lo, i // n_lo] = part[i * piece:(i + 1) * piece, :]
        for e in range(1, n_lo):
            send(pa.at[d, lo_of[e]], ra.at[d, lo], sa1.at[d, e], va1.at[d, lo], c, hi * n_lo + lo_of[e])
        part = jnp.dot(attbuf[zz], w2[1], preferred_element_type=F32).astype(BF16)
        for i in range(n_h):
            pb[d, i // n_lo, i % n_lo] = part[i * piece:(i + 1) * piece, :]
        send(pb.at[d, 1 - hi], rb.at[d], sb1.at[d], vb1.at[d], c, (1 - hi) * n_lo + lo)

    def second(d):
        total = pa[d, lo].astype(F32)
        for e in range(1, n_lo):
            ll = lo_of[e]
            remote(pa.at[d, ll], ra.at[d, ll], sa1.at[d, e], va1.at[d, ll], c, hi * n_lo + ll).wait_recv()
            total = total + ra[d, ll].astype(F32)
        ta[d] = total.astype(BF16)
        send(ta.at[d, 1 - hi], qa2.at[d], sa2.at[d], va2.at[d], c, (1 - hi) * n_lo + lo)
        remote(pb.at[d, hi], rb.at[d], sb1.at[d], vb1.at[d], c, (1 - hi) * n_lo + lo).wait_recv()
        tb[d] = (pb[d, hi].astype(F32) + rb[d].astype(F32)).astype(BF16)
        for e in range(1, n_lo):
            send(tb.at[d, lo_of[e]], qb2.at[d, lo], sb2.at[d, e], vb2.at[d, lo], c, hi * n_lo + lo_of[e])

    def third(d):
        remote(ta.at[d, hi], qa2.at[d], sa2.at[d], va2.at[d], c, (1 - hi) * n_lo + lo).wait_recv()
        first = (ta[d, hi].astype(F32) + qa2[d].astype(F32)).astype(BF16)
        total = tb[d, lo].astype(F32)
        for e in range(1, n_lo):
            ll = lo_of[e]
            remote(tb.at[d, ll], qb2.at[d, ll], sb2.at[d, e], vb2.at[d, ll], c, hi * n_lo + ll).wait_recv()
            total = total + qb2[d, ll].astype(F32)
        if d == 0:
            zbuf[z, :, 0:width] = first
            zbuf[z, :, width:] = total.astype(BF16)
        else:
            rbuf[d, :, 0:width] = first
            rbuf[d, :, width:] = total.astype(BF16)
            send(rbuf.at[d], zbuf.at[z], zs.at[d], zr.at[z], c_of[d], h)

    def deliver(d):
        zz = z_of[(n_z - d) % n_z]
        if d > 0:
            remote(rbuf.at[0], zbuf.at[zz], zs.at[0], zr.at[zz], partner, h).wait_recv()

        @pl.when(zz != h)
        def _():
            remote(zbuf.at[zz], out.at[h], os_.at[d], or_.at[h], c, zz).start()

        @pl.when(zz == h)
        def _():
            out[h] = zbuf[zz]

    def delivered(d):
        zz = z_of[(n_z - d) % n_z]

        @pl.when(zz != h)
        def _():
            remote(zbuf.at[zz], out.at[h], os_.at[d], or_.at[h], c, zz).wait_send()

    for d in range(n_z + 3):
        if d < n_z:
            project(d)
        if 1 <= d <= n_z:
            second(d - 1)
        if 2 <= d <= n_z + 1:
            third(d - 2)
        if d >= 3:
            deliver(d - 3)
    for e in range(1, n_h):
        hh = h_of[e]
        remote(zbuf.at[0], out.at[hh], os_.at[0], or_.at[hh], c, hh).wait_recv()
    for d in range(n_z):
        delivered(d)
    for copy in sends:
        copy.wait_send()


def shards(n_c, n_h, q_latent, latent_cache, w_q_up, w_kv_up, w_out, token_pos, start_offset):
    rows, q_block = q_latent.shape
    heads = w_q_up.shape[1] // (NOPE + ROPE)
    n_z, n_lo = n_c // 2, n_h // 2
    assert n_z == n_h
    keys = n_c * rows
    width = w_out.shape[1]
    piece = rows // n_h
    absolute = (token_pos + start_offset[0]).astype(F32)
    freqs = rope_base ** (-jnp.arange(ROPE // 2, dtype=F32) * 2.0 / ROPE)
    angle = absolute[:, None] * freqs[None, :]
    cosine, sine = jnp.cos(angle), jnp.sin(angle)
    cos = jnp.concatenate([cosine, cosine], axis=1)
    sin = jnp.concatenate([-sine, sine], axis=1)
    kpos = jnp.broadcast_to(token_pos.astype(F32)[None, :], (8, rows))
    dma = pltpu.SemaphoreType.DMA
    anywhere = pl.BlockSpec(memory_space=pltpu.HBM)
    vmem = pl.BlockSpec(memory_space=pltpu.VMEM)
    result = pl.pallas_call(
        functools.partial(kernel, n_c, n_h, heads, rows),
        out_shape=jax.ShapeDtypeStruct((n_h, piece, 2 * width), BF16),
        in_specs=[anywhere] * 5 + [vmem] * 3,
        out_specs=vmem,
        scratch_shapes=[
            pltpu.VMEM(w_q_up.shape, BF16),
            pltpu.VMEM(w_kv_up.shape, BF16),
            pltpu.VMEM((2,) + w_out.shape, BF16),
            pltpu.VMEM((n_h, rows, q_block), BF16),
            pltpu.VMEM((n_c, LANES, rows), BF16),
            pltpu.VMEM((2, n_z, 8, rows), F32),
            pltpu.VMEM((heads * rows, LANES), BF16),
            pltpu.VMEM((heads * rows, keys), F32),
            pltpu.VMEM((heads * rows, keys), BF16),
            pltpu.VMEM((n_z, rows, heads * VDIM), BF16),
            pltpu.VMEM((n_z, n_lo, 2, piece, width), BF16),
            pltpu.VMEM((n_z, n_lo, 2, piece, width), BF16),
            pltpu.VMEM((n_z, 2, piece, width), BF16),
            pltpu.VMEM((n_z, piece, width), BF16),
            pltpu.VMEM((n_z, 2, n_lo, piece, width), BF16),
            pltpu.VMEM((n_z, n_lo, piece, width), BF16),
            pltpu.VMEM((n_z, n_lo, piece, width), BF16),
            pltpu.VMEM((n_z, n_lo, piece, width), BF16),
            pltpu.VMEM((n_z, piece, 2 * width), BF16),
            pltpu.VMEM((n_z, piece, 2 * width), BF16),
            dma((5,)),
            dma((n_h,)), dma((n_h,)),
            dma((n_z,)), dma((n_z,)), dma((n_c,)),
            dma((n_z,)), dma((n_z,)), dma((n_z,)), dma((n_z,)),
            dma((n_z,)), dma((n_z,)), dma, dma,
            dma, dma,
            dma((n_z,)), dma((n_z,)),
            dma((n_z, n_lo)), dma((n_z, n_lo)), dma((n_z,)), dma((n_z,)),
            dma((n_z,)), dma((n_z,)), dma((n_z, n_lo)), dma((n_z, n_lo)),
            dma((n_z,)), dma((n_z,)),
            dma((n_z,)), dma((n_h,)),
        ],
        compiler_params=pltpu.CompilerParams(
            collective_id=0, has_side_effects=True, vmem_limit_bytes=67043328 - (768 << 10)
        ),
        name="mla",
    )(q_latent, latent_cache.T, w_q_up, w_kv_up, w_out, cos, sin, kpos)
    return result.reshape(rows, 2 * width)


def solution(mesh):
    in_specs = (
        P("ctx", "head"),
        P("ctx", None),
        P(None, "head"),
        P(None, "head"),
        P("head", "ctx"),
        P("ctx"),
        P(),
    )
    out_specs = P("ctx", "head")
    body = functools.partial(shards, mesh.shape["ctx"], mesh.shape["head"])
    return jax.shard_map(body, mesh=mesh, in_specs=in_specs, out_specs=out_specs, check_vma=False)
```

profile of v0, /device:TPU:24, one launch (start us, length us, event | category | flops | bytes accessed | tf_op | source)
XLA Modules:
  0.0 62.8 jit_solution(17611043971957233660)
XLA Ops:
  0.7 0.7 %fusion.1 = (f32[128]{0:T(128)S(1)}, f32[128]{0:T(128)S(1)}) fusion(s32[128]{0:T(128)} %param.12, s32[]{:T(128)} %bitcast.3), kind=kLoop, calls=%fused_computation.7 | loop fusion | flops 384 | bytes 1540 | tf_op jit(solution)/shard_map/convert_element_type | solution.py:266
  1.4 0.6 broadcast_in_dim.2.kpos
  2.0 0.3 fusion
  2.3 0.8 %pad_maximum_fusion = (f32[128,64]{1,0:T(8,128)}, f32[128,64]{1,0:T(8,128)}) fusion(f32[128,32]{1,0:T(8,128)S(1)} %get-tuple-element.7, f32[128,32]{1,0:T(8,128)S(1)} %get-tuple-element.6, f32[128,32]{1,0:T(8,128)S(1)} %get-tuple-element.5), kind=kLoop, calls=%fused_computation.2 | loop fusion | flops 16384 | bytes 114688 | tf_op jit(solution)/shard_map/concatenate | solution.py:264
  3.1 57.9 %mla.1 = bf16[4,32,1792]{2,1,0:T(8,128)(2,1)} custom-call(bf16[128,384]{1,0:T(8,128)(2,1)} %qlat.1, bf16[576,128]{1,0:T(8,128)(2,1)} %bitcast.5, bf16[1536,768]{1,0:T(8,128)(2,1)} %wq.1, bf16[512,1024]{1,0:T(8,128)(2,1)} %wkv.1, bf16[512,896]{1,0:T(8,128)(2,1)} %wout.1, f32[128,64]{1,0:T(8,128)} %get-tuple-element.10.cos, f32[128,64]{1,0:T(8,128)} %get-tuple-element.11.sin, ...), custom_call_target="tpu_custom_call" | custom-call | tf_op jit(solution)/shard_map/mla/pallas_call | solution.py:270
  61.0 1.8 %copy.11 = bf16[128,1792]{1,0:T(8,128)(2,1)} copy(bf16[128,1792]{1,0:T(8,128)(2,1)} %bitcast.4) | data formatting | bytes 917504
  (1 shorter events, 0.0 us)
where the time goes:
time: 63 us; the launch traced here: 62.8 us
  Pallas kernels  57.9 us (92%)
  local copies, waits for them, and re-layouts  2.41 us (4%)
  other arithmetic  1.81 us (3%)
  between operations  0.67 us (1%)
    pallas_call x1, Pallas kernels, shards(): pl.pallas_call(functools.partial(kernel, n_c, n_h, heads, rows), out_shap...  57.9 us
    unnamed x1, local copies, waits for them, and re-layouts  1.82 us

commit v1 on v0

--- a/solution.py
+++ b/solution.py
@@ -2,6 +2,7 @@
 
 import jax
 import jax.numpy as jnp
+import numpy as np
 from jax import lax
 from jax.experimental import pallas as pl
 from jax.experimental.pallas import tpu as pltpu
@@ -27,9 +28,9 @@
 
 def kernel(
     n_c, n_h, heads, rows,
-    qlat, lat, wq, wkv, wout, cos, sin, kpos,
+    qlat, lat, wq, wkv, wout, tok_h, freq_h, offset_h,
     out,
-    wq_v, wkv_v, w2, qbuf, latbuf, posbuf, qa, score, prob, attbuf,
+    tok, freq, offset, wq_v, wkv_v, w2, qbuf, latbuf, posbuf, qa, score, prob, attbuf,
     pa, ra, ta, qa2, pb, rb, tb, qb2, rbuf, zbuf,
     lsem, qs, qr, lzs, lps, latr, xzs, xzr, xps, xpr, pzs, pzr, pps, ppr, ws, wr, ats, atr,
     sa1, va1, sa2, va2, sb1, vb1, sb2, vb2, zs, zr, os_, or_,
@@ -72,6 +73,9 @@
         pltpu.make_async_copy(wkv, wkv_v, lsem.at[2]),
         pltpu.make_async_copy(lat, slot(c), lsem.at[3]),
         pltpu.make_async_copy(wout, w2.at[k], lsem.at[4]),
+        pltpu.make_async_copy(tok_h, tok, lsem.at[5]),
+        pltpu.make_async_copy(freq_h, freq, lsem.at[6]),
+        pltpu.make_async_copy(offset_h, offset, lsem.at[7]),
     ]
     for copy in local:
         copy.start()
@@ -97,14 +101,23 @@
     for d in range(n_z - 1, 0, -1):
         send(lat.at[both, :], latbuf.at[c, both, :], lzs.at[d], latr.at[c], c_of[d], h)
     send(lat, slot(c), lps.at[0], latr.at[c], partner, h)
-    posbuf[k, z] = kpos[...]
-    for d in range(1, n_z):
-        send(kpos, posbuf.at[k, z], pzs.at[d], pzr.at[z], c_of[d], h)
+    for d in range(1, n_z):
+        send(tok_h, posbuf.at[k, z], pzs.at[d], pzr.at[z], c_of[d], h)
+    for copy in local[5:]:
+        copy.wait()
+    posbuf[k, z] = tok[...]
 
     for d in range(1, n_z):
         cc = c_of[d]
         remote(lat.at[mine, :], latbuf.at[cc, mine, :], xzs.at[d], xzr.at[z_of[d]], cc, h).wait_recv()
         send(latbuf.at[cc, mine, :], latbuf.at[cc, mine, :], xps.at[d], xpr.at[z_of[d]], c, pair)
+
+    positions = jnp.transpose(jnp.broadcast_to(tok[...].astype(F32), (8, rows)))[:, 0:1]
+    absolute = jnp.transpose(jnp.broadcast_to((tok[...] + offset[...]).astype(F32), (8, rows)))[:, 0:1]
+    angle = absolute * freq[...]
+    cosine, sine = jnp.cos(angle), jnp.sin(angle)
+    cos = jnp.concatenate([cosine, cosine], axis=1)
+    sin = jnp.concatenate([-sine, sine], axis=1)
 
     local[0].wait()
     local[1].wait()
@@ -124,7 +137,7 @@
         rope = query[:, base + NOPE:base + NOPE + ROPE]
         half = ROPE // 2
         swapped = jnp.concatenate([rope[:, half:], rope[:, :half]], axis=1)
-        rotated = rope * cos[...] + swapped * sin[...]
+        rotated = rope * cos + swapped * sin
         qa[lines, KVL:LANES] = rotated.astype(BF16)
 
     for d in range(1, n_z):
@@ -135,7 +148,7 @@
         ).wait_recv()
         send(slot(c_of[d]), slot(c_of[d]), lps.at[d], latr.at[c_of[d]], partner, h)
     for d in range(1, n_z):
-        remote(kpos, posbuf.at[k, z_of[d]], pzs.at[d], pzr.at[z_of[d]], c_of[d], h).wait_recv()
+        remote(tok, posbuf.at[k, z_of[d]], pzs.at[d], pzr.at[z_of[d]], c_of[d], h).wait_recv()
     send(posbuf.at[k], posbuf.at[k], pps, ppr, partner, h)
     send(wout, w2.at[k], ws, wr, partner, h)
     local[3].wait()
@@ -144,10 +157,10 @@
         remote(lat, slot(cc), lps.at[d], latr.at[cc], partner, h).wait_recv()
 
     remote(posbuf.at[1 - k], posbuf.at[1 - k], pps, ppr, partner, h).wait_recv()
-    key_pos = jnp.concatenate([posbuf[cc % 2, cc // 2, 0:1, :] for cc in range(n_c)], axis=1)
+    key_pos = jnp.concatenate([posbuf[cc % 2, cc // 2] for cc in range(n_c)], axis=1).astype(F32)
     latents = jnp.concatenate([latbuf[cc] for cc in range(n_c)], axis=1)
     score[...] = jnp.dot(qa[...], latents, preferred_element_type=F32)
-    visible = key_pos <= jnp.transpose(kpos[...])[:, 0:1]
+    visible = key_pos <= positions
     sums = []
     for j in range(heads):
         lines = slice(j * rows, (j + 1) * rows)
@@ -257,28 +270,25 @@
     keys = n_c * rows
     width = w_out.shape[1]
     piece = rows // n_h
-    absolute = (token_pos + start_offset[0]).astype(F32)
-    freqs = rope_base ** (-jnp.arange(ROPE // 2, dtype=F32) * 2.0 / ROPE)
-    angle = absolute[:, None] * freqs[None, :]
-    cosine, sine = jnp.cos(angle), jnp.sin(angle)
-    cos = jnp.concatenate([cosine, cosine], axis=1)
-    sin = jnp.concatenate([-sine, sine], axis=1)
-    kpos = jnp.broadcast_to(token_pos.astype(F32)[None, :], (8, rows))
+    freqs = rope_base ** (-np.arange(ROPE // 2) * 2.0 / ROPE)
     dma = pltpu.SemaphoreType.DMA
     anywhere = pl.BlockSpec(memory_space=pltpu.HBM)
     vmem = pl.BlockSpec(memory_space=pltpu.VMEM)
     result = pl.pallas_call(
         functools.partial(kernel, n_c, n_h, heads, rows),
-        out_shape=jax.ShapeDtypeStruct((n_h, piece, 2 * width), BF16),
-        in_specs=[anywhere] * 5 + [vmem] * 3,
+        out_shape=pltpu.VMEM((n_h, piece, 2 * width), BF16),
+        in_specs=[anywhere] * 8,
         out_specs=vmem,
         scratch_shapes=[
+            pltpu.VMEM((1, rows), jnp.int32),
+            pltpu.VMEM((1, ROPE // 2), F32),
+            pltpu.VMEM((1, 1), jnp.int32),
             pltpu.VMEM(w_q_up.shape, BF16),
             pltpu.VMEM(w_kv_up.shape, BF16),
             pltpu.VMEM((2,) + w_out.shape, BF16),
             pltpu.VMEM((n_h, rows, q_block), BF16),
             pltpu.VMEM((n_c, LANES, rows), BF16),
-            pltpu.VMEM((2, n_z, 8, rows), F32),
+            pltpu.VMEM((2, n_z, 1, rows), jnp.int32),
             pltpu.VMEM((heads * rows, LANES), BF16),
             pltpu.VMEM((heads * rows, keys), F32),
             pltpu.VMEM((heads * rows, keys), BF16),
@@ -293,7 +303,7 @@
             pltpu.VMEM((n_z, n_lo, piece, width), BF16),
             pltpu.VMEM((n_z, piece, 2 * width), BF16),
             pltpu.VMEM((n_z, piece, 2 * width), BF16),
-            dma((5,)),
+            dma((8,)),
             dma((n_h,)), dma((n_h,)),
             dma((n_z,)), dma((n_z,)), dma((n_c,)),
             dma((n_z,)), dma((n_z,)), dma((n_z,)), dma((n_z,)),
@@ -309,7 +319,7 @@
             collective_id=0, has_side_effects=True, vmem_limit_bytes=67043328 - (768 << 10)
         ),
         name="mla",
-    )(q_latent, latent_cache.T, w_q_up, w_kv_up, w_out, cos, sin, kpos)
+    )(q_latent, latent_cache.T, w_q_up, w_kv_up, w_out, token_pos[None, :], freqs.astype(np.float32)[None, :], start_offset[None, :])
     return result.reshape(rows, 2 * width)
 
 

time: 63 us -> 57.8 us (0.917)
  other arithmetic: 1.81 us -> 0 us
  Pallas kernels: 57.9 us -> 56.2 us
  local copies, waits for them, and re-layouts: 2.41 us -> 0.77 us
    pallas_call x1, Pallas kernels: 57.9 us -> 56.2 us  [shards(): pl.pallas_call(functools.partial(kernel, n_c, n_h, heads, rows), out_shap...]
    unnamed x1, local copies, waits for them, and re-layouts: 1.82 us -> 0.77 us
    concatenate x1 -> x0, other arithmetic: 0.75 us -> none  [shards(): cos = jnp.concatenate([cosine, cosine], axis=1)]
    convert_element_type x1 -> x0, other arithmetic: 0.74 us -> none  [shards(): kpos = jnp.broadcast_to(token_pos.astype(F32)[None, :], (8, rows))]
where the time goes in v1:
time: 57.8 us; the launch traced here: 57.6 us
  Pallas kernels  56.2 us (97%)
  local copies, waits for them, and re-layouts  0.77 us (1%)
  between operations  0.66 us (1%)
    pallas_call x1, Pallas kernels, shards(): pl.pallas_call(functools.partial(kernel, n_c, n_h, heads, rows), out_shap...  56.2 us

profile of v1, /device:TPU:24, one launch (start us, length us, event | category | flops | bytes accessed | tf_op | source)
XLA Modules:
  0.0 57.6 jit_solution(9449353793861932744)
XLA Ops:
  0.7 56.2 %mla.1 = bf16[4,32,1792]{2,1,0:T(8,128)(2,1)S(1)} custom-call(bf16[128,384]{1,0:T(8,128)(2,1)} %qlat.1, bf16[576,128]{1,0:T(8,128)(2,1)} %bitcast.6, bf16[1536,768]{1,0:T(8,128)(2,1)} %wq.1, bf16[512,1024]{1,0:T(8,128)(2,1)} %wkv.1, bf16[512,896]{1,0:T(8,128)(2,1)} %wout.1, s32[1,128]{1,0:T(1,128)} %bitcast.7, f32[1,32]{1,0:T(1,128)} %constant.2.clone.freq_h, ...), custom_call_target="tpu_custom_call" | custom-call | tf_op jit(solution)/shard_map/mla/pallas_call | solution.py:277
  56.9 0.8 %copy.10 = bf16[128,1792]{1,0:T(8,128)(2,1)} copy(bf16[128,1792]{1,0:T(8,128)(2,1)S(1)} %bitcast.5) | data formatting | bytes 917504

commit v2 on v1

--- a/solution.py
+++ b/solution.py
@@ -31,9 +31,9 @@
     qlat, lat, wq, wkv, wout, tok_h, freq_h, offset_h,
     out,
     tok, freq, offset, wq_v, wkv_v, w2, qbuf, latbuf, posbuf, qa, score, prob, attbuf,
-    pa, ra, ta, qa2, pb, rb, tb, qb2, rbuf, zbuf,
+    pa, ra, ta, qa2, pb, rb, tb, qb2, rbuf,
     lsem, qs, qr, lzs, lps, latr, xzs, xzr, xps, xpr, pzs, pzr, pps, ppr, ws, wr, ats, atr,
-    sa1, va1, sa2, va2, sb1, vb1, sb2, vb2, zs, zr, os_, or_,
+    sa1, va1, sa2, va2, sb1, vb1, sb2, vb2, os_, or_,
 ):
     n_z = n_c // 2
     piece = rows // n_h
@@ -216,48 +216,40 @@
             ll = lo_of[e]
             remote(tb.at[d, ll], qb2.at[d, ll], sb2.at[d, e], vb2.at[d, ll], c, hi * n_lo + ll).wait_recv()
             total = total + qb2[d, ll].astype(F32)
+        rbuf[d, :, 0:width] = first
+        rbuf[d, :, width:] = total.astype(BF16)
         if d == 0:
-            zbuf[z, :, 0:width] = first
-            zbuf[z, :, width:] = total.astype(BF16)
+            @pl.when(z != h)
+            def _():
+                deliver(d).start()
+
+            @pl.when(z == h)
+            def _():
+                out[h] = rbuf[d]
         else:
-            rbuf[d, :, 0:width] = first
-            rbuf[d, :, width:] = total.astype(BF16)
-            send(rbuf.at[d], zbuf.at[z], zs.at[d], zr.at[z], c_of[d], h)
+            deliver(d).start()
 
     def deliver(d):
-        zz = z_of[(n_z - d) % n_z]
-        if d > 0:
-            remote(rbuf.at[0], zbuf.at[zz], zs.at[0], zr.at[zz], partner, h).wait_recv()
-
-        @pl.when(zz != h)
-        def _():
-            remote(zbuf.at[zz], out.at[h], os_.at[d], or_.at[h], c, zz).start()
-
-        @pl.when(zz == h)
-        def _():
-            out[h] = zbuf[zz]
-
-    def delivered(d):
-        zz = z_of[(n_z - d) % n_z]
-
-        @pl.when(zz != h)
-        def _():
-            remote(zbuf.at[zz], out.at[h], os_.at[d], or_.at[h], c, zz).wait_send()
-
-    for d in range(n_z + 3):
+        return remote(rbuf.at[d], out.at[h], os_.at[d], or_.at[h], c_of[d], z)
+
+    for d in range(n_z + 2):
         if d < n_z:
             project(d)
         if 1 <= d <= n_z:
             second(d - 1)
-        if 2 <= d <= n_z + 1:
+        if d >= 2:
             third(d - 2)
-        if d >= 3:
-            deliver(d - 3)
-    for e in range(1, n_h):
-        hh = h_of[e]
-        remote(zbuf.at[0], out.at[hh], os_.at[0], or_.at[hh], c, hh).wait_recv()
+    for hh in range(n_h):
+        @pl.when((z != h) | (h != hh))
+        def _():
+            remote(rbuf.at[0], out.at[hh], os_.at[0], or_.at[hh], c, h).wait_recv()
     for d in range(n_z):
-        delivered(d)
+        if d > 0:
+            deliver(d).wait_send()
+        else:
+            @pl.when(z != h)
+            def _():
+                deliver(d).wait_send()
     for copy in sends:
         copy.wait_send()
 
@@ -302,7 +294,6 @@
             pltpu.VMEM((n_z, n_lo, piece, width), BF16),
             pltpu.VMEM((n_z, n_lo, piece, width), BF16),
             pltpu.VMEM((n_z, piece, 2 * width), BF16),
-            pltpu.VMEM((n_z, piece, 2 * width), BF16),
             dma((8,)),
             dma((n_h,)), dma((n_h,)),
             dma((n_z,)), dma((n_z,)), dma((n_c,)),
@@ -312,7 +303,6 @@
             dma((n_z,)), dma((n_z,)),
             dma((n_z, n_lo)), dma((n_z, n_lo)), dma((n_z,)), dma((n_z,)),
             dma((n_z,)), dma((n_z,)), dma((n_z, n_lo)), dma((n_z, n_lo)),
-            dma((n_z,)), dma((n_z,)),
             dma((n_z,)), dma((n_h,)),
         ],
         compiler_params=pltpu.CompilerParams(

time: 57.8 us -> 58.9 us (1.019)
  Pallas kernels: 56.2 us -> 57.3 us
    pallas_call x1, Pallas kernels: 56.2 us -> 57.3 us  [shards(): pl.pallas_call(functools.partial(kernel, n_c, n_h, heads, rows), out_shap...]
where the time goes in v2:
time: 58.9 us; the launch traced here: 58.7 us
  Pallas kernels  57.3 us (97%)
  local copies, waits for them, and re-layouts  0.77 us (1%)
  between operations  0.66 us (1%)
    pallas_call x1, Pallas kernels, shards(): pl.pallas_call(functools.partial(kernel, n_c, n_h, heads, rows), out_shap...  57.3 us

profile of v2, /device:TPU:24, one launch (start us, length us, event | category | flops | bytes accessed | tf_op | source)
XLA Modules:
  0.0 58.7 jit_solution(1363535925186922727)
XLA Ops:
  0.7 57.3 %mla.1 = bf16[4,32,1792]{2,1,0:T(8,128)(2,1)S(1)} custom-call(bf16[128,384]{1,0:T(8,128)(2,1)} %qlat.1, bf16[576,128]{1,0:T(8,128)(2,1)} %bitcast.6, bf16[1536,768]{1,0:T(8,128)(2,1)} %wq.1, bf16[512,1024]{1,0:T(8,128)(2,1)} %wkv.1, bf16[512,896]{1,0:T(8,128)(2,1)} %wout.1, s32[1,128]{1,0:T(1,128)} %bitcast.7, f32[1,32]{1,0:T(1,128)} %constant.2.clone.freq_h, ...), custom_call_target="tpu_custom_call" | custom-call | tf_op jit(solution)/shard_map/mla/pallas_call | solution.py:269
  57.9 0.8 %copy.10 = bf16[128,1792]{1,0:T(8,128)(2,1)} copy(bf16[128,1792]{1,0:T(8,128)(2,1)S(1)} %bitcast.5) | data formatting | bytes 917504

commit v3 on v2

v3 whole, which is shorter than its diff:
```python
import functools

import jax
import jax.numpy as jnp
import numpy as np
from jax import lax
from jax.experimental import pallas as pl
from jax.experimental.pallas import tpu as pltpu
from jax.sharding import PartitionSpec as P

KVL = 512
NOPE = 128
ROPE = 64
VDIM = 128
LANES = KVL + ROPE

negative_fill = -1e30
softmax_scale = 0.135
rope_base = 10000.0
F32 = jnp.float32
BF16 = jnp.bfloat16
MESH = pl.DeviceIdType.MESH
gather_lag, reduce_lag = 4, 8


def dot_t(a, b):
    return lax.dot_general(a, b, (((1,), (1,)), ((), ())), preferred_element_type=F32)


def kernel(
    n_c, n_h, heads, rows, parts,
    qlat, lat, wq, wkv, wout, tok_h, freq_h, offset_h,
    out,
    tok, freq, offset, wq_v, wkv_v, w2, qbuf, latbuf, posbuf, qa, score, prob, attbuf,
    pa, ra, rbuf,
    lsem, qs, qr, lzs, lps, latr, xzs, xzr, xps, xpr, pzs, pzr, pps, ppr, ws, wr, ats, atr,
    gs, gr, rs, rr, os_, or_,
):
    n_z = n_c // 2
    n_lo = n_h // 2
    span = rows // parts
    piece = span // n_lo
    depth, width = wout.shape
    q_block = qbuf.shape[2]
    c = lax.axis_index("ctx")
    h = lax.axis_index("head")
    k = lax.rem(c, 2)
    z = lax.div(c, 2)
    partner = c + 1 - 2 * k
    z_of = [lax.rem(z + d, n_z) for d in range(n_z)]
    h_of = [lax.rem(h + e, n_h) for e in range(n_h)]
    shorter = jnp.minimum(z, n_z - 1 - z)
    slots = []
    for i in range(n_z):
        even = z - (i + 1) // 2 if i % 2 else z + i // 2
        single = jnp.where(2 * z < n_z, z + i - shorter, z - i + shorter)
        slots.append(jnp.where(i <= 2 * shorter, even, single))
    hi, lo = lax.div(h, n_lo), lax.rem(h, n_lo)
    lo_of = [lax.rem(lo + e, n_lo) for e in range(n_lo)]
    c_of = [2 * zz + k for zz in z_of]

    def remote(src, dst, ssem, rsem, cc, hh):
        return pltpu.make_async_remote_copy(
            src_ref=src, dst_ref=dst, send_sem=ssem, recv_sem=rsem,
            device_id=(cc, hh), device_id_type=MESH,
        )

    def slot(cc):
        return latbuf.at[cc]

    barrier = pltpu.get_barrier_semaphore()
    for d in range(1, n_z):
        pl.semaphore_signal(barrier, inc=1, device_id=(c_of[d], h), device_id_type=MESH)
    for e in range(1, n_h):
        pl.semaphore_signal(barrier, inc=1, device_id=(c, h_of[e]), device_id_type=MESH)
    pl.semaphore_signal(barrier, inc=1, device_id=(partner, h), device_id_type=MESH)

    local = [
        pltpu.make_async_copy(qlat, qbuf.at[h], lsem.at[0]),
        pltpu.make_async_copy(wq, wq_v, lsem.at[1]),
        pltpu.make_async_copy(wkv, wkv_v, lsem.at[2]),
        pltpu.make_async_copy(lat, slot(c), lsem.at[3]),
        pltpu.make_async_copy(tok_h, tok, lsem.at[4]),
        pltpu.make_async_copy(freq_h, freq, lsem.at[5]),
        pltpu.make_async_copy(offset_h, offset, lsem.at[6]),
    ]
    for copy in local:
        copy.start()
    keeps = k == hi
    across = (1 - hi) * n_lo + lo
    own_rows, other_rows = w2.at[0:depth, :], w2.at[depth:2 * depth, :]
    kept = pltpu.make_async_copy(wout, own_rows, lsem.at[7])
    pl.when(keeps)(kept.start)
    pl.semaphore_wait(barrier, n_z + n_h - 1)

    third_rows = LANES // 3
    odd = lax.rem(lo, 2)
    pair = hi * n_lo + lo + 1 - 2 * odd
    mine = pl.ds(pl.multiple_of(odd * third_rows, third_rows), third_rows)
    other = pl.ds(pl.multiple_of((1 - odd) * third_rows, third_rows), third_rows)
    both = pl.ds(2 * third_rows, third_rows)
    sends = []

    passed = []

    def send(*args):
        copy = remote(*args)
        copy.start()
        sends.append(copy)

    def start_if(ok, copy):
        pl.when(ok)(copy.start)
        passed.append((ok, copy))

    for e in range(1, n_h):
        send(qlat, qbuf.at[h], qs.at[e], qr.at[h], c, h_of[e])
    start_if(jnp.logical_not(keeps), remote(wout, other_rows, ws.at[0], wr.at[1], c, across))
    for d in range(n_z - 1, 0, -1):
        send(lat.at[mine, :], latbuf.at[c, mine, :], xzs.at[d], xzr.at[z], c_of[d], h)
    for d in range(n_z - 1, 0, -1):
        send(lat.at[both, :], latbuf.at[c, both, :], lzs.at[d], latr.at[c], c_of[d], h)
    send(lat, slot(c), lps.at[0], latr.at[c], partner, h)
    for d in range(1, n_z):
        send(tok_h, posbuf.at[k, z], pzs.at[d], pzr.at[z], c_of[d], h)
    for copy in local[4:]:
        copy.wait()
    posbuf[k, z] = tok[...]

    for d in range(1, n_z):
        cc = c_of[d]
        remote(lat.at[mine, :], latbuf.at[cc, mine, :], xzs.at[d], xzr.at[z_of[d]], cc, h).wait_recv()
        send(latbuf.at[cc, mine, :], latbuf.at[cc, mine, :], xps.at[d], xpr.at[z_of[d]], c, pair)

    positions = jnp.transpose(jnp.broadcast_to(tok[...].astype(F32), (8, rows)))[:, 0:1]
    absolute = jnp.transpose(jnp.broadcast_to((tok[...] + offset[0]).astype(F32), (8, rows)))[:, 0:1]
    angle = absolute * freq[...]
    cosine, sine = jnp.cos(angle), jnp.sin(angle)
    cos = jnp.concatenate([cosine, cosine], axis=1)
    sin = jnp.concatenate([-sine, sine], axis=1)

    local[0].wait()
    local[1].wait()
    for e in range(1, n_h):
        remote(qlat, qbuf.at[h_of[e]], qs.at[e], qr.at[h_of[e]], c, h_of[e]).wait_recv()
    query = None
    for g in range(n_h):
        term = jnp.dot(qbuf[g], wq_v[g * q_block:(g + 1) * q_block, :], preferred_element_type=F32)
        query = term if query is None else query + term
    local[2].wait()
    for j in range(heads):
        base = j * (NOPE + ROPE)
        nope = query[:, base:base + NOPE].astype(BF16)
        main = dot_t(nope, wkv_v[:, j * 256:j * 256 + NOPE])
        lines = slice(j * rows, (j + 1) * rows)
        qa[lines, 0:KVL] = main.astype(BF16)
        rope = query[:, base + NOPE:base + NOPE + ROPE]
        half = ROPE // 2
        swapped = jnp.concatenate([rope[:, half:], rope[:, :half]], axis=1)
        rotated = rope * cos + swapped * sin
        qa[lines, KVL:LANES] = rotated.astype(BF16)

    for d in range(1, n_z):
        cc = c_of[d]
        remote(lat.at[both, :], latbuf.at[cc, both, :], lzs.at[d], latr.at[cc], cc, h).wait_recv()
        remote(
            latbuf.at[cc, other, :], latbuf.at[cc, other, :], xps.at[d], xpr.at[z_of[d]], c, pair
        ).wait_recv()
        send(slot(c_of[d]), slot(c_of[d]), lps.at[d], latr.at[c_of[d]], partner, h)
    for d in range(1, n_z):
        remote(tok, posbuf.at[k, z_of[d]], pzs.at[d], pzr.at[z_of[d]], c_of[d], h).wait_recv()
    send(posbuf.at[k], posbuf.at[k], pps, ppr, partner, h)
    start_if(keeps, remote(wout, own_rows, ws.at[1], wr.at[0], partner, h))
    local[3].wait()
    for d in range(n_z):
        cc = 2 * z_of[d] + 1 - k
        remote(lat, slot(cc), lps.at[d], latr.at[cc], partner, h).wait_recv()

    remote(posbuf.at[1 - k], posbuf.at[1 - k], pps, ppr, partner, h).wait_recv()
    key_pos = jnp.concatenate([posbuf[cc % 2, cc // 2] for cc in range(n_c)], axis=1).astype(F32)
    latents = jnp.concatenate([latbuf[cc] for cc in range(n_c)], axis=1)
    score[...] = jnp.dot(qa[...], latents, preferred_element_type=F32)
    visible = key_pos <= positions
    sums = []
    for j in range(heads):
        lines = slice(j * rows, (j + 1) * rows)
        s = jnp.where(visible, score[lines, :] * softmax_scale, negative_fill)
        largest = jnp.max(s, axis=-1, keepdims=True)
        weights = jnp.where(visible, jnp.exp(s - largest), 0.0)
        sums.append(jnp.sum(weights, axis=-1, keepdims=True))
        prob[lines, :] = weights.astype(BF16)
    summed = dot_t(prob[...], latents[0:KVL, :])
    for j in range(heads):
        normed = (summed[j * rows:(j + 1) * rows, :] / sums[j]).astype(BF16)
        value = jnp.dot(normed, wkv_v[:, j * 256 + NOPE:(j + 1) * 256], preferred_element_type=F32)
        attbuf[z, :, j * VDIM:(j + 1) * VDIM] = value.astype(BF16)

    def pass_on(zz, p, row, to):
        lines = attbuf.at[zz, p * span:(p + 1) * span, 0:depth]
        return remote(lines, lines, ats.at[row, p], atr.at[zz, p], 2 * to + k, h)

    for p in range(parts):
        start_if(z + 1 < n_z, pass_on(z, p, 0, z + 1))
        start_if(z > 0, pass_on(z, p, n_z, z - 1))

    def share(d):
        zz, p = slots[d // parts], d % parts
        lines = attbuf.at[zz, p * span:(p + 1) * span, :]
        return remote(
            lines.at[:, 0:depth], lines.at[:, depth:2 * depth], gs.at[d], gr.at[d], c, across
        )

    def arrive(d):
        if d >= parts:
            zz, p = slots[d // parts], d % parts
            onward = jnp.where(zz < z, z + 1, z - 1)
            pass_on(zz, p, d // parts, z).wait_recv()
            start_if((onward >= 0) & (onward < n_z), pass_on(zz, p, d // parts, onward))
        share(d).start()

    def project(d):
        share(d).wait_recv()
        lines = attbuf[slots[d // parts], d % parts * span:(d % parts + 1) * span, :]
        part = jnp.dot(lines, w2[...], preferred_element_type=F32).astype(BF16)
        for i in range(n_lo):
            pa[d, i] = part[i * piece:(i + 1) * piece, :]
        for e in range(1, n_lo):
            send(pa.at[d, lo_of[e]], ra.at[d, lo], rs.at[d, e], rr.at[d, lo], c, hi * n_lo + lo_of[e])

    def place(side, p, line):
        if width % 128:
            return out.at[side, p, line]
        return out.at[p, line, :, pl.ds(pl.multiple_of(side * width, 128), width)]

    def deliver(d):
        return remote(
            rbuf.at[d], place(hi, d % parts, lo), os_.at[d], or_.at[d % parts, h],
            2 * slots[d // parts] + k, z,
        )

    def reduce(d):
        total = pa[d, lo].astype(F32)
        for e in range(1, n_lo):
            ll = lo_of[e]
            remote(pa.at[d, ll], ra.at[d, ll], rs.at[d, e], rr.at[d, ll], c, hi * n_lo + ll).wait_recv()
            total = total + ra[d, ll].astype(F32)
        rbuf[d] = total.astype(BF16)
        if d < parts:
            pl.when(z != h)(deliver(d).start)

            @pl.when(z == h)
            def _():
                place(hi, d % parts, lo)[...] = rbuf[d]
        else:
            deliver(d).start()

    def weights():
        @pl.when(keeps)
        def _():
            kept.wait()
            remote(wout, other_rows, ws.at[0], wr.at[1], c, across).wait_recv()

        start_if(keeps, remote(other_rows, other_rows, ws.at[2], wr.at[1], partner, h))

        @pl.when(jnp.logical_not(keeps))
        def _():
            remote(wout, own_rows, ws.at[1], wr.at[0], partner, h).wait_recv()
            remote(other_rows, other_rows, ws.at[2], wr.at[1], partner, h).wait_recv()

    chunks = n_z * parts
    for d in range(chunks + reduce_lag):
        if d < chunks:
            arrive(d)
        if d == gather_lag:
            weights()
        if 0 <= d - gather_lag < chunks:
            project(d - gather_lag)
        if 0 <= d - reduce_lag < chunks:
            reduce(d - reduce_lag)
    for hh in range(n_h):
        @pl.when((z != h) | (h != hh))
        def _():
            for p in range(parts):
                remote(
                    rbuf.at[0], place(hh // n_lo, p, hh % n_lo), os_.at[0], or_.at[p, hh], c, h
                ).wait_recv()
    for d in range(chunks):
        share(d).wait_send()
        if d >= parts:
            deliver(d).wait_send()
        else:
            pl.when(z != h)(deliver(d).wait_send)
    for ok, copy in passed:
        pl.when(ok)(copy.wait_send)
    for copy in sends:
        copy.wait_send()


def shards(n_c, n_h, q_latent, latent_cache, w_q_up, w_kv_up, w_out, token_pos, start_offset):
    rows, q_block = q_latent.shape
    heads = w_q_up.shape[1] // (NOPE + ROPE)
    n_z, n_lo = n_c // 2, n_h // 2
    assert n_z == n_h
    keys = n_c * rows
    width = w_out.shape[1]
    parts = 2 if rows // n_lo >= 32 else 1
    piece = rows // n_lo // parts
    chunks = n_z * parts
    split = 1 if width % 128 else 0
    freqs = rope_base ** (-np.arange(ROPE // 2) * 2.0 / ROPE)
    dma = pltpu.SemaphoreType.DMA
    anywhere = pl.BlockSpec(memory_space=pltpu.HBM)
    vmem = pl.BlockSpec(memory_space=pltpu.VMEM)
    result = pl.pallas_call(
        functools.partial(kernel, n_c, n_h, heads, rows, parts),
        out_shape=pltpu.VMEM((2,) * split + (parts, n_lo, piece, (2 - split) * width), BF16),
        in_specs=[anywhere] * 8,
        out_specs=vmem,
        scratch_shapes=[
            pltpu.VMEM((1, rows), jnp.int32),
            pltpu.VMEM((1, ROPE // 2), F32),
            pltpu.SMEM((1,), jnp.int32),
            pltpu.VMEM(w_q_up.shape, BF16),
            pltpu.VMEM(w_kv_up.shape, BF16),
            pltpu.VMEM((2 * w_out.shape[0], width), BF16),
            pltpu.VMEM((n_h, rows, q_block), BF16),
            pltpu.VMEM((n_c, LANES, rows), BF16),
            pltpu.VMEM((2, n_z, 1, rows), jnp.int32),
            pltpu.VMEM((heads * rows, LANES), BF16),
            pltpu.VMEM((heads * rows, keys), F32),
            pltpu.VMEM((heads * rows, keys), BF16),
            pltpu.VMEM((n_z, rows, 2 * heads * VDIM), BF16),
            pltpu.VMEM((chunks, n_lo, piece, width), BF16),
            pltpu.VMEM((chunks, n_lo, piece, width), BF16),
            pltpu.VMEM((chunks, piece, width), BF16),
            dma((8,)),
            dma((n_h,)), dma((n_h,)),
            dma((n_z,)), dma((n_z,)), dma((n_c,)),
            dma((n_z,)), dma((n_z,)), dma((n_z,)), dma((n_z,)),
            dma((n_z,)), dma((n_z,)), dma, dma,
            dma((3,)), dma((2,)),
            dma((n_z + 1, parts)), dma((n_z, parts)),
            dma((chunks,)), dma((chunks,)),
            dma((chunks, n_lo)), dma((chunks, n_lo)),
            dma((chunks,)), dma((parts, n_h)),
        ],
        compiler_params=pltpu.CompilerParams(
            collective_id=0, has_side_effects=True, vmem_limit_bytes=67043328 - (768 << 10)
        ),
        name="mla",
    )(q_latent, latent_cache.T, w_q_up, w_kv_up, w_out, token_pos[None, :], freqs.astype(np.float32)[None, :], start_offset)
    if not split:
        return result.reshape(rows, 2 * width)
    result = result.reshape(2, rows, width)
    return jnp.concatenate([result[0], result[1]], axis=1)


def solution(mesh):
    in_specs = (
        P("ctx", "head"),
        P("ctx", None),
        P(None, "head"),
        P(None, "head"),
        P("head", "ctx"),
        P("ctx"),
        P(),
    )
    out_specs = P("ctx", "head")
    body = functools.partial(shards, mesh.shape["ctx"], mesh.shape["head"])
    return jax.shard_map(body, mesh=mesh, in_specs=in_specs, out_specs=out_specs, check_vma=False)
```

time: 58.9 us -> 51 us (0.87)
  Pallas kernels: 57.3 us -> 49.4 us
    pallas_call x1, Pallas kernels: 57.3 us -> 49.4 us  [shards(): pl.pallas_call(functools.partial(kernel, n_c, n_h, heads, rows, parts), o...]
where the time goes in v3:
time: 51 us; the launch traced here: 50.8 us
  Pallas kernels  49.4 us (97%)
  local copies, waits for them, and re-layouts  0.77 us (2%)
  between operations  0.66 us (1%)
    pallas_call x1, Pallas kernels, shards(): pl.pallas_call(functools.partial(kernel, n_c, n_h, heads, rows, parts), o...  49.4 us

profile of v3, /device:TPU:24, one launch (start us, length us, event | category | flops | bytes accessed | tf_op | source)
XLA Modules:
  0.0 50.8 jit_solution(15630891858025001763)
XLA Ops:
  0.7 49.4 %mla.1 = bf16[2,2,32,1792]{3,2,1,0:T(8,128)(2,1)S(1)} custom-call(bf16[128,384]{1,0:T(8,128)(2,1)} %qlat.1, bf16[576,128]{1,0:T(8,128)(2,1)} %bitcast.4, bf16[1536,768]{1,0:T(8,128)(2,1)} %wq.1, bf16[512,1024]{1,0:T(8,128)(2,1)} %wkv.1, bf16[512,896]{1,0:T(8,128)(2,1)} %wout.1, s32[1,128]{1,0:T(1,128)} %bitcast.5, f32[1,32]{1,0:T(1,128)} %constant.2.clone.freq_h, ...), custom_call_target="tpu_custom_call" | custom-call | tf_op jit(solution)/shard_map/mla/pallas_call | solution.py:313
  50.0 0.8 %copy.10 = bf16[128,1792]{1,0:T(8,128)(2,1)} copy(bf16[128,1792]{1,0:T(8,128)(2,1)S(1)} %bitcast.3) | data formatting | bytes 917504

commit v4 on v3

--- a/solution.py
+++ b/solution.py
@@ -20,7 +20,8 @@
 F32 = jnp.float32
 BF16 = jnp.bfloat16
 MESH = pl.DeviceIdType.MESH
-gather_lag, reduce_lag = 4, 8
+strips, early_strips = 4, 1
+gather_lag, reduce_lag = 4, 10
 
 
 def dot_t(a, b):
@@ -93,12 +94,16 @@
     pl.when(keeps)(kept.start)
     pl.semaphore_wait(barrier, n_z + n_h - 1)
 
-    third_rows = LANES // 3
     odd = lax.rem(lo, 2)
-    pair = hi * n_lo + lo + 1 - 2 * odd
-    mine = pl.ds(pl.multiple_of(odd * third_rows, third_rows), third_rows)
-    other = pl.ds(pl.multiple_of((1 - odd) * third_rows, third_rows), third_rows)
-    both = pl.ds(2 * third_rows, third_rows)
+    beside = lo + 1 - 2 * odd
+    peers = [(hi, beside), (1 - hi, lo), (1 - hi, beside)]
+    share_rows = LANES // 36 * 6
+
+    def part_of(a, b):
+        return pl.ds(pl.multiple_of((2 * a + lax.rem(b, 2)) * share_rows, share_rows), share_rows)
+
+    mine = part_of(hi, lo)
+    both = pl.ds(4 * share_rows, LANES - 4 * share_rows)
     sends = []
 
     passed = []
@@ -112,24 +117,52 @@
         pl.when(ok)(copy.start)
         passed.append((ok, copy))
 
-    for e in range(1, n_h):
-        send(qlat, qbuf.at[h], qs.at[e], qr.at[h], c, h_of[e])
-    start_if(jnp.logical_not(keeps), remote(wout, other_rows, ws.at[0], wr.at[1], c, across))
-    for d in range(n_z - 1, 0, -1):
-        send(lat.at[mine, :], latbuf.at[c, mine, :], xzs.at[d], xzr.at[z], c_of[d], h)
-    for d in range(n_z - 1, 0, -1):
-        send(lat.at[both, :], latbuf.at[c, both, :], lzs.at[d], latr.at[c], c_of[d], h)
+    far = across
+    send(qlat, qbuf.at[h], qs.at[0, 0], qr.at[h], c, far)
+    for e in range(1, n_lo):
+        send(qlat, qbuf.at[h], qs.at[0, e], qr.at[h], c, hi * n_lo + lo_of[e])
+
+    def strip(i):
+        return pl.ds(i * (depth // strips), depth // strips)
+
+    def cross(i):
+        return remote(
+            wout.at[strip(i), :], other_rows.at[strip(i), :], ws.at[i], wr.at[1 + i], c, across
+        )
+
+    def hand_on(i):
+        lines = other_rows.at[strip(i), :]
+        pl.when(keeps)(cross(i).wait_recv)
+        start_if(keeps, remote(lines, lines, ws.at[strips + i], wr.at[1 + i], partner, h))
+
+    for i in range(early_strips):
+        start_if(jnp.logical_not(keeps), cross(i))
+    away = z_of[:0:-1]
+    for i, zz in enumerate(away):
+        send(lat.at[mine, :], latbuf.at[c, mine, :], xzs.at[i], xzr.at[z], 2 * zz + k, h)
+    for i, zz in enumerate(away):
+        send(lat.at[both, :], latbuf.at[c, both, :], lzs.at[i], latr.at[c], 2 * zz + k, h)
     send(lat, slot(c), lps.at[0], latr.at[c], partner, h)
-    for d in range(1, n_z):
-        send(tok_h, posbuf.at[k, z], pzs.at[d], pzr.at[z], c_of[d], h)
+    for i, zz in enumerate(away):
+        send(tok_h, posbuf.at[k, z], pzs.at[i], pzr.at[z], 2 * zz + k, h)
     for copy in local[4:]:
         copy.wait()
     posbuf[k, z] = tok[...]
 
-    for d in range(1, n_z):
-        cc = c_of[d]
-        remote(lat.at[mine, :], latbuf.at[cc, mine, :], xzs.at[d], xzr.at[z_of[d]], cc, h).wait_recv()
-        send(latbuf.at[cc, mine, :], latbuf.at[cc, mine, :], xps.at[d], xpr.at[z_of[d]], c, pair)
+    remote(qlat, qbuf.at[far], qs.at[0, 0], qr.at[far], c, far).wait_recv()
+    for e in range(1, n_lo):
+        send(qbuf.at[far], qbuf.at[far], qs.at[1, e], qr.at[far], c, hi * n_lo + lo_of[e])
+
+    for i in range(1, n_z):
+        zz = z_of[i]
+        cc = 2 * zz + k
+        remote(lat.at[mine, :], latbuf.at[cc, mine, :], xzs.at[i - 1], xzr.at[zz], cc, h).wait_recv()
+        for r, (a, b) in enumerate(peers):
+            block = latbuf.at[cc, mine, :]
+            send(block, block, xps.at[i, r], xpr.at[zz, r], c, a * n_lo + b)
+
+    for i in range(early_strips, strips):
+        start_if(jnp.logical_not(keeps), cross(i))
 
     positions = jnp.transpose(jnp.broadcast_to(tok[...].astype(F32), (8, rows)))[:, 0:1]
     absolute = jnp.transpose(jnp.broadcast_to((tok[...] + offset[0]).astype(F32), (8, rows)))[:, 0:1]
@@ -140,8 +173,10 @@
 
     local[0].wait()
     local[1].wait()
-    for e in range(1, n_h):
-        remote(qlat, qbuf.at[h_of[e]], qs.at[e], qr.at[h_of[e]], c, h_of[e]).wait_recv()
+    for e in range(1, n_lo):
+        for a in (hi, 1 - hi):
+            there = a * n_lo + lo_of[e]
+            remote(qlat, qbuf.at[there], qs.at[0, e], qr.at[there], c, there).wait_recv()
     query = None
     for g in range(n_h):
         term = jnp.dot(qbuf[g], wq_v[g * q_block:(g + 1) * q_block, :], preferred_element_type=F32)
@@ -159,23 +194,26 @@
         rotated = rope * cos + swapped * sin
         qa[lines, KVL:LANES] = rotated.astype(BF16)
 
-    for d in range(1, n_z):
-        cc = c_of[d]
-        remote(lat.at[both, :], latbuf.at[cc, both, :], lzs.at[d], latr.at[cc], cc, h).wait_recv()
-        remote(
-            latbuf.at[cc, other, :], latbuf.at[cc, other, :], xps.at[d], xpr.at[z_of[d]], c, pair
-        ).wait_recv()
-        send(slot(c_of[d]), slot(c_of[d]), lps.at[d], latr.at[c_of[d]], partner, h)
-    for d in range(1, n_z):
-        remote(tok, posbuf.at[k, z_of[d]], pzs.at[d], pzr.at[z_of[d]], c_of[d], h).wait_recv()
+    for i in range(1, n_z):
+        zz = z_of[i]
+        remote(tok, posbuf.at[k, zz], pzs.at[i - 1], pzr.at[zz], 2 * zz + k, h).wait_recv()
     send(posbuf.at[k], posbuf.at[k], pps, ppr, partner, h)
-    start_if(keeps, remote(wout, own_rows, ws.at[1], wr.at[0], partner, h))
+    for i in range(1, n_z):
+        zz = z_of[i]
+        cc = 2 * zz + k
+        remote(lat.at[both, :], latbuf.at[cc, both, :], lzs.at[i - 1], latr.at[cc], cc, h).wait_recv()
+        for r, (a, b) in enumerate(peers):
+            block = latbuf.at[cc, part_of(a, b), :]
+            remote(block, block, xps.at[i, r], xpr.at[zz, r], c, a * n_lo + b).wait_recv()
+        send(slot(cc), slot(cc), lps.at[i], latr.at[cc], partner, h)
+    start_if(keeps, remote(wout, own_rows, ws.at[2 * strips], wr.at[0], partner, h))
     local[3].wait()
-    for d in range(n_z):
-        cc = 2 * z_of[d] + 1 - k
-        remote(lat, slot(cc), lps.at[d], latr.at[cc], partner, h).wait_recv()
-
+    for i in range(n_z):
+        cc = 2 * z_of[i] + 1 - k
+        remote(lat, slot(cc), lps.at[i], latr.at[cc], partner, h).wait_recv()
     remote(posbuf.at[1 - k], posbuf.at[1 - k], pps, ppr, partner, h).wait_recv()
+    for i in range(2):
+        hand_on(i)
     key_pos = jnp.concatenate([posbuf[cc % 2, cc // 2] for cc in range(n_c)], axis=1).astype(F32)
     latents = jnp.concatenate([latbuf[cc] for cc in range(n_c)], axis=1)
     score[...] = jnp.dot(qa[...], latents, preferred_element_type=F32)
@@ -254,17 +292,16 @@
             deliver(d).start()
 
     def weights():
-        @pl.when(keeps)
-        def _():
-            kept.wait()
-            remote(wout, other_rows, ws.at[0], wr.at[1], c, across).wait_recv()
-
-        start_if(keeps, remote(other_rows, other_rows, ws.at[2], wr.at[1], partner, h))
+        pl.when(keeps)(kept.wait)
+        for i in range(2, strips):
+            hand_on(i)
 
         @pl.when(jnp.logical_not(keeps))
         def _():
-            remote(wout, own_rows, ws.at[1], wr.at[0], partner, h).wait_recv()
-            remote(other_rows, other_rows, ws.at[2], wr.at[1], partner, h).wait_recv()
+            remote(wout, own_rows, ws.at[2 * strips], wr.at[0], partner, h).wait_recv()
+            for i in range(strips):
+                lines = other_rows.at[strip(i), :]
+                remote(lines, lines, ws.at[strips + i], wr.at[1 + i], partner, h).wait_recv()
 
     chunks = n_z * parts
     for d in range(chunks + reduce_lag):
@@ -333,11 +370,11 @@
             pltpu.VMEM((chunks, n_lo, piece, width), BF16),
             pltpu.VMEM((chunks, piece, width), BF16),
             dma((8,)),
-            dma((n_h,)), dma((n_h,)),
+            dma((2, n_lo)), dma((n_h,)),
             dma((n_z,)), dma((n_z,)), dma((n_c,)),
-            dma((n_z,)), dma((n_z,)), dma((n_z,)), dma((n_z,)),
+            dma((n_z,)), dma((n_z,)), dma((n_z, 3)), dma((n_z, 3)),
             dma((n_z,)), dma((n_z,)), dma, dma,
-            dma((3,)), dma((2,)),
+            dma((2 * strips + 1,)), dma((1 + strips,)),
             dma((n_z + 1, parts)), dma((n_z, parts)),
             dma((chunks,)), dma((chunks,)),
             dma((chunks, n_lo)), dma((chunks, n_lo)),

time: 51 us -> 49.2 us (0.965)
  Pallas kernels: 49.4 us -> 47.6 us
    pallas_call x1, Pallas kernels: 49.4 us -> 47.6 us  [shards(): pl.pallas_call(functools.partial(kernel, n_c, n_h, heads, rows, parts), o...]
where the time goes in v4:
time: 49.2 us; the launch traced here: 49 us
  Pallas kernels  47.6 us (97%)
  local copies, waits for them, and re-layouts  0.77 us (2%)
  between operations  0.66 us (1%)
    pallas_call x1, Pallas kernels, shards(): pl.pallas_call(functools.partial(kernel, n_c, n_h, heads, rows, parts), o...  47.6 us

profile of v4, /device:TPU:24, one launch (start us, length us, event | category | flops | bytes accessed | tf_op | source)
XLA Modules:
  0.0 49.0 jit_solution(13330829797891441370)
XLA Ops:
  0.7 47.6 %mla.1 = bf16[2,2,32,1792]{3,2,1,0:T(8,128)(2,1)S(1)} custom-call(bf16[128,384]{1,0:T(8,128)(2,1)} %qlat.1, bf16[576,128]{1,0:T(8,128)(2,1)} %bitcast.4, bf16[1536,768]{1,0:T(8,128)(2,1)} %wq.1, bf16[512,1024]{1,0:T(8,128)(2,1)} %wkv.1, bf16[512,896]{1,0:T(8,128)(2,1)} %wout.1, s32[1,128]{1,0:T(1,128)} %bitcast.5, f32[1,32]{1,0:T(1,128)} %constant.2.clone.freq_h, ...), custom_call_target="tpu_custom_call" | custom-call | tf_op jit(solution)/shard_map/mla/pallas_call | solution.py:350
  48.2 0.8 %copy.10 = bf16[128,1792]{1,0:T(8,128)(2,1)} copy(bf16[128,1792]{1,0:T(8,128)(2,1)S(1)} %bitcast.3) | data formatting | bytes 917504

commit v5 on v4

--- a/solution.py
+++ b/solution.py
@@ -21,7 +21,7 @@
 BF16 = jnp.bfloat16
 MESH = pl.DeviceIdType.MESH
 strips, early_strips = 4, 1
-gather_lag, reduce_lag = 4, 10
+gather_lag, reduce_lag = 4, 11
 
 
 def dot_t(a, b):
@@ -97,7 +97,7 @@
     odd = lax.rem(lo, 2)
     beside = lo + 1 - 2 * odd
     peers = [(hi, beside), (1 - hi, lo), (1 - hi, beside)]
-    share_rows = LANES // 36 * 6
+    share_rows = LANES // 36 * 5
 
     def part_of(a, b):
         return pl.ds(pl.multiple_of((2 * a + lax.rem(b, 2)) * share_rows, share_rows), share_rows)
@@ -196,16 +196,16 @@
 
     for i in range(1, n_z):
         zz = z_of[i]
-        remote(tok, posbuf.at[k, zz], pzs.at[i - 1], pzr.at[zz], 2 * zz + k, h).wait_recv()
-    send(posbuf.at[k], posbuf.at[k], pps, ppr, partner, h)
-    for i in range(1, n_z):
-        zz = z_of[i]
         cc = 2 * zz + k
         remote(lat.at[both, :], latbuf.at[cc, both, :], lzs.at[i - 1], latr.at[cc], cc, h).wait_recv()
         for r, (a, b) in enumerate(peers):
             block = latbuf.at[cc, part_of(a, b), :]
             remote(block, block, xps.at[i, r], xpr.at[zz, r], c, a * n_lo + b).wait_recv()
         send(slot(cc), slot(cc), lps.at[i], latr.at[cc], partner, h)
+    for i in range(1, n_z):
+        zz = z_of[i]
+        remote(tok, posbuf.at[k, zz], pzs.at[i - 1], pzr.at[zz], 2 * zz + k, h).wait_recv()
+    send(posbuf.at[k], posbuf.at[k], pps, ppr, partner, h)
     start_if(keeps, remote(wout, own_rows, ws.at[2 * strips], wr.at[0], partner, h))
     local[3].wait()
     for i in range(n_z):
@@ -223,7 +223,7 @@
         lines = slice(j * rows, (j + 1) * rows)
         s = jnp.where(visible, score[lines, :] * softmax_scale, negative_fill)
         largest = jnp.max(s, axis=-1, keepdims=True)
-        weights = jnp.where(visible, jnp.exp(s - largest), 0.0)
+        weights = jnp.exp(s - largest)
         sums.append(jnp.sum(weights, axis=-1, keepdims=True))
         prob[lines, :] = weights.astype(BF16)
     summed = dot_t(prob[...], latents[0:KVL, :])

time: 49.2 us -> 48.5 us (0.986)
  Pallas kernels: 47.6 us -> 46.9 us
    pallas_call x1, Pallas kernels: 47.6 us -> 46.9 us  [shards(): pl.pallas_call(functools.partial(kernel, n_c, n_h, heads, rows, parts), o...]
where the time goes in v5:
time: 48.5 us; the launch traced here: 48.3 us
  Pallas kernels  46.9 us (97%)
  local copies, waits for them, and re-layouts  0.77 us (2%)
  between operations  0.66 us (1%)
    pallas_call x1, Pallas kernels, shards(): pl.pallas_call(functools.partial(kernel, n_c, n_h, heads, rows, parts), o...  46.9 us

profile of v5, /device:TPU:24, one launch (start us, length us, event | category | flops | bytes accessed | tf_op | source)
XLA Modules:
  0.0 48.3 jit_solution(14312243753487830234)
XLA Ops:
  0.7 46.9 %mla.1 = bf16[2,2,32,1792]{3,2,1,0:T(8,128)(2,1)S(1)} custom-call(bf16[128,384]{1,0:T(8,128)(2,1)} %qlat.1, bf16[576,128]{1,0:T(8,128)(2,1)} %bitcast.4, bf16[1536,768]{1,0:T(8,128)(2,1)} %wq.1, bf16[512,1024]{1,0:T(8,128)(2,1)} %wkv.1, bf16[512,896]{1,0:T(8,128)(2,1)} %wout.1, s32[1,128]{1,0:T(1,128)} %bitcast.5, f32[1,32]{1,0:T(1,128)} %constant.2.clone.freq_h, ...), custom_call_target="tpu_custom_call" | custom-call | tf_op jit(solution)/shard_map/mla/pallas_call | solution.py:350
  47.5 0.8 %copy.10 = bf16[128,1792]{1,0:T(8,128)(2,1)} copy(bf16[128,1792]{1,0:T(8,128)(2,1)S(1)} %bitcast.3) | data formatting | bytes 917504

commit v6 on v5

--- a/solution.py
+++ b/solution.py
@@ -118,6 +118,7 @@
         passed.append((ok, copy))
 
     far = across
+    send(lat, slot(c), lps.at[0], latr.at[c], partner, h)
     send(qlat, qbuf.at[h], qs.at[0, 0], qr.at[h], c, far)
     for e in range(1, n_lo):
         send(qlat, qbuf.at[h], qs.at[0, e], qr.at[h], c, hi * n_lo + lo_of[e])
@@ -137,12 +138,11 @@
 
     for i in range(early_strips):
         start_if(jnp.logical_not(keeps), cross(i))
-    away = z_of[:0:-1]
+    away = slots[1:]
     for i, zz in enumerate(away):
         send(lat.at[mine, :], latbuf.at[c, mine, :], xzs.at[i], xzr.at[z], 2 * zz + k, h)
     for i, zz in enumerate(away):
         send(lat.at[both, :], latbuf.at[c, both, :], lzs.at[i], latr.at[c], 2 * zz + k, h)
-    send(lat, slot(c), lps.at[0], latr.at[c], partner, h)
     for i, zz in enumerate(away):
         send(tok_h, posbuf.at[k, z], pzs.at[i], pzr.at[z], 2 * zz + k, h)
     for copy in local[4:]:
@@ -154,7 +154,7 @@
         send(qbuf.at[far], qbuf.at[far], qs.at[1, e], qr.at[far], c, hi * n_lo + lo_of[e])
 
     for i in range(1, n_z):
-        zz = z_of[i]
+        zz = slots[i]
         cc = 2 * zz + k
         remote(lat.at[mine, :], latbuf.at[cc, mine, :], xzs.at[i - 1], xzr.at[zz], cc, h).wait_recv()
         for r, (a, b) in enumerate(peers):
@@ -186,16 +186,17 @@
         base = j * (NOPE + ROPE)
         nope = query[:, base:base + NOPE].astype(BF16)
         main = dot_t(nope, wkv_v[:, j * 256:j * 256 + NOPE])
-        lines = slice(j * rows, (j + 1) * rows)
-        qa[lines, 0:KVL] = main.astype(BF16)
         rope = query[:, base + NOPE:base + NOPE + ROPE]
         half = ROPE // 2
         swapped = jnp.concatenate([rope[:, half:], rope[:, :half]], axis=1)
         rotated = rope * cos + swapped * sin
-        qa[lines, KVL:LANES] = rotated.astype(BF16)
+        for p in range(parts):
+            lines = slice((p * heads + j) * span, (p * heads + j + 1) * span)
+            qa[lines, 0:KVL] = main[p * span:(p + 1) * span].astype(BF16)
+            qa[lines, KVL:LANES] = rotated[p * span:(p + 1) * span].astype(BF16)
 
     for i in range(1, n_z):
-        zz = z_of[i]
+        zz = slots[i]
         cc = 2 * zz + k
         remote(lat.at[both, :], latbuf.at[cc, both, :], lzs.at[i - 1], latr.at[cc], cc, h).wait_recv()
         for r, (a, b) in enumerate(peers):
@@ -203,42 +204,22 @@
             remote(block, block, xps.at[i, r], xpr.at[zz, r], c, a * n_lo + b).wait_recv()
         send(slot(cc), slot(cc), lps.at[i], latr.at[cc], partner, h)
     for i in range(1, n_z):
-        zz = z_of[i]
+        zz = slots[i]
         remote(tok, posbuf.at[k, zz], pzs.at[i - 1], pzr.at[zz], 2 * zz + k, h).wait_recv()
     send(posbuf.at[k], posbuf.at[k], pps, ppr, partner, h)
     start_if(keeps, remote(wout, own_rows, ws.at[2 * strips], wr.at[0], partner, h))
     local[3].wait()
     for i in range(n_z):
-        cc = 2 * z_of[i] + 1 - k
+        cc = 2 * slots[i] + 1 - k
         remote(lat, slot(cc), lps.at[i], latr.at[cc], partner, h).wait_recv()
     remote(posbuf.at[1 - k], posbuf.at[1 - k], pps, ppr, partner, h).wait_recv()
     for i in range(2):
         hand_on(i)
     key_pos = jnp.concatenate([posbuf[cc % 2, cc // 2] for cc in range(n_c)], axis=1).astype(F32)
     latents = jnp.concatenate([latbuf[cc] for cc in range(n_c)], axis=1)
-    score[...] = jnp.dot(qa[...], latents, preferred_element_type=F32)
-    visible = key_pos <= positions
-    sums = []
-    for j in range(heads):
-        lines = slice(j * rows, (j + 1) * rows)
-        s = jnp.where(visible, score[lines, :] * softmax_scale, negative_fill)
-        largest = jnp.max(s, axis=-1, keepdims=True)
-        weights = jnp.exp(s - largest)
-        sums.append(jnp.sum(weights, axis=-1, keepdims=True))
-        prob[lines, :] = weights.astype(BF16)
-    summed = dot_t(prob[...], latents[0:KVL, :])
-    for j in range(heads):
-        normed = (summed[j * rows:(j + 1) * rows, :] / sums[j]).astype(BF16)
-        value = jnp.dot(normed, wkv_v[:, j * 256 + NOPE:(j + 1) * 256], preferred_element_type=F32)
-        attbuf[z, :, j * VDIM:(j + 1) * VDIM] = value.astype(BF16)
-
     def pass_on(zz, p, row, to):
         lines = attbuf.at[zz, p * span:(p + 1) * span, 0:depth]
         return remote(lines, lines, ats.at[row, p], atr.at[zz, p], 2 * to + k, h)
-
-    for p in range(parts):
-        start_if(z + 1 < n_z, pass_on(z, p, 0, z + 1))
-        start_if(z > 0, pass_on(z, p, n_z, z - 1))
 
     def share(d):
         zz, p = slots[d // parts], d % parts
@@ -247,13 +228,34 @@
             lines.at[:, 0:depth], lines.at[:, depth:2 * depth], gs.at[d], gr.at[d], c, across
         )
 
+    score[...] = jnp.dot(qa[...], latents, preferred_element_type=F32)
+    for p in range(parts):
+        visible = key_pos <= positions[p * span:(p + 1) * span]
+        sums = []
+        for j in range(heads):
+            lines = slice((p * heads + j) * span, (p * heads + j + 1) * span)
+            s = jnp.where(visible, score[lines, :] * softmax_scale, negative_fill)
+            largest = jnp.max(s, axis=-1, keepdims=True)
+            weights = jnp.exp(s - largest)
+            sums.append(jnp.sum(weights, axis=-1, keepdims=True))
+            prob[lines, :] = weights.astype(BF16)
+        lines = slice(p * heads * span, (p + 1) * heads * span)
+        summed = dot_t(prob[lines, :], latents[0:KVL, :])
+        for j in range(heads):
+            normed = (summed[j * span:(j + 1) * span, :] / sums[j]).astype(BF16)
+            value = jnp.dot(normed, wkv_v[:, j * 256 + NOPE:(j + 1) * 256], preferred_element_type=F32)
+            attbuf[z, p * span:(p + 1) * span, j * VDIM:(j + 1) * VDIM] = value.astype(BF16)
+        start_if(z + 1 < n_z, pass_on(z, p, 0, z + 1))
+        start_if(z > 0, pass_on(z, p, n_z, z - 1))
+        share(p).start()
+
     def arrive(d):
         if d >= parts:
             zz, p = slots[d // parts], d % parts
             onward = jnp.where(zz < z, z + 1, z - 1)
             pass_on(zz, p, d // parts, z).wait_recv()
             start_if((onward >= 0) & (onward < n_z), pass_on(zz, p, d // parts, onward))
-        share(d).start()
+            share(d).start()
 
     def project(d):
         share(d).wait_recv()

time: 48.5 us -> 48.1 us (level)
  no operation moved by 1% of the time
where the time goes in v6:
time: 48.1 us; the launch traced here: 47.9 us
  Pallas kernels  46.5 us (97%)
  local copies, waits for them, and re-layouts  0.77 us (2%)
  between operations  0.66 us (1%)
    pallas_call x1, Pallas kernels, shards(): pl.pallas_call(functools.partial(kernel, n_c, n_h, heads, rows, parts), o...  46.5 us

profile of v6, /device:TPU:24, one launch (start us, length us, event | category | flops | bytes accessed | tf_op | source)
XLA Modules:
  0.0 47.9 jit_solution(12155796413984799547)
XLA Ops:
  0.7 46.5 %mla.1 = bf16[2,2,32,1792]{3,2,1,0:T(8,128)(2,1)S(1)} custom-call(bf16[128,384]{1,0:T(8,128)(2,1)} %qlat.1, bf16[576,128]{1,0:T(8,128)(2,1)} %bitcast.4, bf16[1536,768]{1,0:T(8,128)(2,1)} %wq.1, bf16[512,1024]{1,0:T(8,128)(2,1)} %wkv.1, bf16[512,896]{1,0:T(8,128)(2,1)} %wout.1, s32[1,128]{1,0:T(1,128)} %bitcast.5, f32[1,32]{1,0:T(1,128)} %constant.2.clone.freq_h, ...), custom_call_target="tpu_custom_call" | custom-call | tf_op jit(solution)/shard_map/mla/pallas_call | solution.py:352
  47.2 0.8 %copy.10 = bf16[128,1792]{1,0:T(8,128)(2,1)} copy(bf16[128,1792]{1,0:T(8,128)(2,1)S(1)} %bitcast.3) | data formatting | bytes 917504

commit v7 on v6

--- a/solution.py
+++ b/solution.py
@@ -164,6 +164,8 @@
     for i in range(early_strips, strips):
         start_if(jnp.logical_not(keeps), cross(i))
 
+    start_if(keeps, remote(wout, own_rows, ws.at[2 * strips], wr.at[0], partner, h))
+
     positions = jnp.transpose(jnp.broadcast_to(tok[...].astype(F32), (8, rows)))[:, 0:1]
     absolute = jnp.transpose(jnp.broadcast_to((tok[...] + offset[0]).astype(F32), (8, rows)))[:, 0:1]
     angle = absolute * freq[...]
@@ -207,7 +209,6 @@
         zz = slots[i]
         remote(tok, posbuf.at[k, zz], pzs.at[i - 1], pzr.at[zz], 2 * zz + k, h).wait_recv()
     send(posbuf.at[k], posbuf.at[k], pps, ppr, partner, h)
-    start_if(keeps, remote(wout, own_rows, ws.at[2 * strips], wr.at[0], partner, h))
     local[3].wait()
     for i in range(n_z):
         cc = 2 * slots[i] + 1 - k

time: 48.1 us -> 48.1 us (level)
  no operation moved by 1% of the time
where the time goes in v7:
time: 48.1 us; the launch traced here: 47.9 us
  Pallas kernels  46.5 us (97%)
  local copies, waits for them, and re-layouts  0.77 us (2%)
  between operations  0.66 us (1%)
    pallas_call x1, Pallas kernels, shards(): pl.pallas_call(functools.partial(kernel, n_c, n_h, heads, rows, parts), o...  46.5 us

profile of v7, /device:TPU:24, one launch (start us, length us, event | category | flops | bytes accessed | tf_op | source)
XLA Modules:
  0.0 47.9 jit_solution(14820336314802992097)
XLA Ops:
  0.7 46.5 %mla.1 = bf16[2,2,32,1792]{3,2,1,0:T(8,128)(2,1)S(1)} custom-call(bf16[128,384]{1,0:T(8,128)(2,1)} %qlat.1, bf16[576,128]{1,0:T(8,128)(2,1)} %bitcast.4, bf16[1536,768]{1,0:T(8,128)(2,1)} %wq.1, bf16[512,1024]{1,0:T(8,128)(2,1)} %wkv.1, bf16[512,896]{1,0:T(8,128)(2,1)} %wout.1, s32[1,128]{1,0:T(1,128)} %bitcast.5, f32[1,32]{1,0:T(1,128)} %constant.2.clone.freq_h, ...), custom_call_target="tpu_custom_call" | custom-call | tf_op jit(solution)/shard_map/mla/pallas_call | solution.py:353
  47.2 0.8 %copy.10 = bf16[128,1792]{1,0:T(8,128)(2,1)} copy(bf16[128,1792]{1,0:T(8,128)(2,1)S(1)} %bitcast.3) | data formatting | bytes 917504

commit v8 on v7

--- a/solution.py
+++ b/solution.py
@@ -21,7 +21,7 @@
 BF16 = jnp.bfloat16
 MESH = pl.DeviceIdType.MESH
 strips, early_strips = 4, 1
-gather_lag, reduce_lag = 4, 11
+gather_lag, reduce_lag = 4, 10
 
 
 def dot_t(a, b):

time: 48.1 us -> 48.1 us (level)
  no operation moved by 1% of the time
where the time goes in v8:
time: 48.1 us; the launch traced here: 47.9 us
  Pallas kernels  46.5 us (97%)
  local copies, waits for them, and re-layouts  0.77 us (2%)
  between operations  0.66 us (1%)
    pallas_call x1, Pallas kernels, shards(): pl.pallas_call(functools.partial(kernel, n_c, n_h, heads, rows, parts), o...  46.5 us

profile of v8, /device:TPU:24, one launch (start us, length us, event | category | flops | bytes accessed | tf_op | source)
XLA Modules:
  0.0 47.9 jit_solution(17800402568978846460)
XLA Ops:
  0.7 46.5 %mla.1 = bf16[2,2,32,1792]{3,2,1,0:T(8,128)(2,1)S(1)} custom-call(bf16[128,384]{1,0:T(8,128)(2,1)} %qlat.1, bf16[576,128]{1,0:T(8,128)(2,1)} %bitcast.4, bf16[1536,768]{1,0:T(8,128)(2,1)} %wq.1, bf16[512,1024]{1,0:T(8,128)(2,1)} %wkv.1, bf16[512,896]{1,0:T(8,128)(2,1)} %wout.1, s32[1,128]{1,0:T(1,128)} %bitcast.5, f32[1,32]{1,0:T(1,128)} %constant.2.clone.freq_h, ...), custom_call_target="tpu_custom_call" | custom-call | tf_op jit(solution)/shard_map/mla/pallas_call | solution.py:353
  47.2 0.8 %copy.10 = bf16[128,1792]{1,0:T(8,128)(2,1)} copy(bf16[128,1792]{1,0:T(8,128)(2,1)S(1)} %bitcast.3) | data formatting | bytes 917504
